TPU v7x, 32 devices: a whole 2x2x4 slice. The times are simulated.
32 devices in a mesh: dev: 8 (over z, x), ma: 4 (over y, core).
Axes of the slice: x: 2, y: 2, z: 4, core: 2. Of those that a mesh axis runs over, the one named last changes fastest.
Arguments:
- inputs: bfloat16 [8192, 2048], P('ma', 'dev'), may hold values from -6 to 6
- cotangent: bfloat16 [8192, 2048], P('ma', 'dev'), may hold values from -6 to 6
- factors: bfloat16 [4, 64, 16384], P(None, 'ma', 'dev'), may hold values from -0.5 to 0.5
- exponents: int32 [4, 64], P(None, 'ma'), may hold values from -6 to -4
- error_buffer: bfloat16 [8, 4, 64, 16384], P('dev', None, 'ma'), may hold values from -96 to 96
Outputs:
- output: bfloat16 [8192, 2048], P('ma', 'dev')
- input_grad: bfloat16 [8192, 2048], P('ma', 'dev')
- grad_mean: float32 [4, 64, 16384], P(None, 'ma', 'dev')
- new_error: bfloat16 [8, 4, 64, 16384], P('dev', None, 'ma')
All inputs are finite; a program needn't handle non-finite values.
Results may differ from a plain program's by a relative error of at most 0.0057.
Values may be sent and summed in bfloat16 or wider, within the bound.
A program may use at most 64 MiB of HBM per device.

v0:
```python
import jax
import jax.numpy as jnp
from jax import lax
from jax.sharding import PartitionSpec as P

B = 128
code_limit = 127.0


def regroup(stacked):
    groups = lax.axis_size("ma")
    count, local_blocks, width, tok_count = stacked.shape
    folded = stacked.reshape(
        count, local_blocks, width // (groups * local_blocks), groups, local_blocks, tok_count
    )
    shaped = jnp.transpose(folded, (0, 4, 2, 3, 1, 5))
    arrived = lax.all_to_all(shaped, "ma", split_axis=3, concat_axis=3, tiled=True)
    return arrived.reshape(count, local_blocks, width, tok_count)


def block_forward(weights, values):
    return jnp.einsum("ncd,nct->ndt", weights, values, preferred_element_type=jnp.float32)


def block_backward(weights, values):
    return jnp.einsum("ncd,ndt->nct", weights, values, preferred_element_type=jnp.float32)


def outer_sum(left, right):
    return jnp.einsum("nct,ndt->ncd", left, right, preferred_element_type=jnp.float32)


def quantize(gradients, error_part, exponent_part):
    totals = gradients.reshape(gradients.shape[:-2] + (-1,)) + error_part.astype(jnp.float32)
    scale_inverse = jnp.left_shift(jnp.ones_like(exponent_part), -exponent_part).astype(
        jnp.float32
    )[..., None]
    code_values = jnp.clip(totals * scale_inverse, -code_limit, code_limit)
    return (code_values, (totals - code_values / scale_inverse).astype(jnp.bfloat16), scale_inverse)


def body(inputs, cotangent, factors, exponents, error_buffer):
    local_blocks = factors.shape[1]
    tok_count = inputs.shape[1]
    group_count = lax.axis_size("dev")
    gathered = lax.all_gather(factors, "dev", axis=2, tiled=True)
    matrices = gathered.reshape(gathered.shape[0], local_blocks, B, B)
    block_in = inputs.reshape(local_blocks, B, tok_count)
    block_cot = cotangent.reshape(local_blocks, B, tok_count)
    first_out = block_forward(matrices[0], block_in).astype(jnp.bfloat16)
    mixed_one = regroup(first_out[None])[0]
    second_out = block_forward(matrices[1], mixed_one).astype(jnp.bfloat16)
    pre_gelu = regroup(second_out[None])[0]
    hidden_wide, gelu_back = jax.vjp(jax.nn.gelu, pre_gelu.astype(jnp.float32))
    hidden = hidden_wide.astype(jnp.bfloat16)
    third_out = block_forward(matrices[2], hidden).astype(jnp.bfloat16)
    mixed_two = regroup(third_out[None])[0]
    fourth_out = block_forward(matrices[3], mixed_two).astype(jnp.bfloat16)
    returned = regroup(fourth_out[None])[0]
    output = (block_in.astype(jnp.float32) + returned.astype(jnp.float32)).astype(jnp.bfloat16)
    back_four = regroup(block_cot[None])[0]
    d_mixed_two = block_backward(matrices[3], back_four).astype(jnp.bfloat16)
    gradient_three = outer_sum(mixed_two, back_four)
    d_third = regroup(d_mixed_two[None])[0]
    d_pre = gelu_back(block_backward(matrices[2], d_third))[0].astype(jnp.bfloat16)
    gradient_two = outer_sum(hidden, d_third)
    d_second = regroup(d_pre[None])[0]
    d_mixed_one = block_backward(matrices[1], d_second).astype(jnp.bfloat16)
    gradient_one = outer_sum(mixed_one, d_second)
    d_first = regroup(d_mixed_one[None])[0]
    input_grad = (block_cot.astype(jnp.float32) + block_backward(matrices[0], d_first)).astype(
        jnp.bfloat16
    )
    gradient_zero = outer_sum(block_in, d_first)
    gradients = jnp.stack([gradient_zero, gradient_one, gradient_two, gradient_three])
    code_values, new_part, scale_inverse = quantize(gradients, error_buffer[0], exponents)
    summed = lax.psum_scatter(code_values, "dev", scatter_dimension=2, tiled=True)
    grad_mean = summed / scale_inverse / group_count
    new_error = new_part[None]
    return (
        output.reshape(local_blocks * B, tok_count),
        input_grad.reshape(local_blocks * B, tok_count),
        grad_mean,
        new_error,
    )


def solution(mesh):
    in_specs = (
        P("ma", "dev"),
        P("ma", "dev"),
        P(None, "ma", "dev"),
        P(None, "ma"),
        P("dev", None, "ma", None),
    )
    out_specs = (P("ma", "dev"), P("ma", "dev"), P(None, "ma", "dev"), P("dev", None, "ma", None))
    return jax.shard_map(body, mesh=mesh, in_specs=in_specs, out_specs=out_specs, check_vma=False)
```

profile of v0, /device:TPU:0, one launch (start us, length us, event | category | flops | bytes accessed | tf_op | source)
XLA Modules:
  0.0 293.5 jit_solution(14815720484470332092)
XLA Ops:
  7.9 2.8 copy.67
  10.7 4.3 %all-to-all-start.4 = ((bf16[1,16,2,4,16,256]{5,4,2,1,0,3:T(8,128)(2,1)}), bf16[1,16,2,4,16,256]{5,4,2,1,0,3:T(8,128)(2,1)S(1)}, u32[]{:S(2)}, u32[]{:S(2)}) async-start(bf16[1,16,2,4,16,256]{5,4,2,1,0,3:T(8,128)(2,1)} %copy.67), calls=%async_computation.4 | async-start | bytes 2097152 | tf_op jit(solution)/shard_map/all_to_all | solution.py:17
  14.9 47.0 %all-gather.2.cloned.1.call-done = bf16[4,16,16384]{2,1,0:T(8,128)(2,1)} async-done(((bf16[4,16,2048]{2,1,0:T(8,128)(2,1)}), bf16[4,16,16384]{2,1,0:T(8,128)(2,1)}) %all-gather.2.cloned.1.call-update) | async-done | bytes 2097168 | tf_op jit(solution)/shard_map/all_gather | solution.py:46
  62.0 2.7 slice_bitcast_fusion
  67.2 4.2 %all-to-all-start = ((bf16[1,16,2,4,16,256]{5,1,2,4,0,3:T(8,128)(2,1)}), bf16[1,16,2,4,16,256]{5,1,2,4,0,3:T(8,128)(2,1)}, u32[]{:S(2)}, u32[]{:S(2)}) async-start(bf16[1,16,2,4,16,256]{5,1,2,4,0,3:T(8,128)(2,1)} %bitcast.115), calls=%async_computation | async-start | bytes 2097152 | tf_op jit(solution)/shard_map/all_to_all | solution.py:17
  74.9 11.0 %all-to-all-done = bf16[1,16,2,4,16,256]{5,1,2,4,0,3:T(8,128)(2,1)} async-done(((bf16[1,16,2,4,16,256]{5,1,2,4,0,3:T(8,128)(2,1)}), bf16[1,16,2,4,16,256]{5,1,2,4,0,3:T(8,128)(2,1)}, u32[]{:S(2)}, u32[]{:S(2)}) %all-to-all-start) | async-done | bytes 1048608 | tf_op jit(solution)/shard_map/all_to_all | solution.py:17
  85.9 4.2 %all-to-all-start.5 = ((bf16[1,16,2,4,16,256]{5,1,2,4,0,3:T(8,128)(2,1)}), bf16[1,16,2,4,16,256]{5,1,2,4,0,3:T(8,128)(2,1)}, u32[]{:S(2)}, u32[]{:S(2)}) async-start(bf16[1,16,2,4,16,256]{5,1,2,4,0,3:T(8,128)(2,1)} %bitcast.111), calls=%async_computation.5 | async-start | bytes 2097152 | tf_op jit(solution)/shard_map/all_to_all | solution.py:17
  90.3 2.0 copy.57
  93.9 10.8 %all-to-all-done.5 = bf16[1,16,2,4,16,256]{5,1,2,4,0,3:T(8,128)(2,1)} async-done(((bf16[1,16,2,4,16,256]{5,1,2,4,0,3:T(8,128)(2,1)}), bf16[1,16,2,4,16,256]{5,1,2,4,0,3:T(8,128)(2,1)}, u32[]{:S(2)}, u32[]{:S(2)}) %all-to-all-start.5) | async-done | bytes 1048608 | tf_op jit(solution)/shard_map/all_to_all | solution.py:17
  104.7 4.2 %all-to-all-start.1 = ((bf16[1,16,2,4,16,256]{5,1,2,4,0,3:T(8,128)(2,1)}), bf16[1,16,2,4,16,256]{5,1,2,4,0,3:T(8,128)(2,1)}, u32[]{:S(2)}, u32[]{:S(2)}) async-start(bf16[1,16,2,4,16,256]{5,1,2,4,0,3:T(8,128)(2,1)} %bitcast.138), calls=%async_computation.1 | async-start | bytes 2097152 | tf_op jit(solution)/shard_map/all_to_all | solution.py:17
  108.9 1.9 copy.83
  110.9 2.8 copy.70
  113.6 9.8 %all-to-all-done.1 = bf16[1,16,2,4,16,256]{5,1,2,4,0,3:T(8,128)(2,1)} async-done(((bf16[1,16,2,4,16,256]{5,1,2,4,0,3:T(8,128)(2,1)}), bf16[1,16,2,4,16,256]{5,1,2,4,0,3:T(8,128)(2,1)}, u32[]{:S(2)}, u32[]{:S(2)}) %all-to-all-start.1) | async-done | bytes 1048608 | tf_op jit(solution)/shard_map/all_to_all | solution.py:17
  123.4 2.0 copy.60
  128.1 4.2 %all-to-all-start.6 = ((bf16[1,16,2,4,16,256]{5,1,2,4,0,3:T(8,128)(2,1)}), bf16[1,16,2,4,16,256]{5,1,2,4,0,3:T(8,128)(2,1)}, u32[]{:S(2)}, u32[]{:S(2)}) async-start(bf16[1,16,2,4,16,256]{5,1,2,4,0,3:T(8,128)(2,1)} %bitcast.140), calls=%async_computation.6 | async-start | bytes 2097152 | tf_op jit(solution)/shard_map/all_to_all | solution.py:17
  132.4 2.6 convolution_convert_fusion.3
  136.1 10.8 %all-to-all-done.6 = bf16[1,16,2,4,16,256]{5,1,2,4,0,3:T(8,128)(2,1)} async-done(((bf16[1,16,2,4,16,256]{5,1,2,4,0,3:T(8,128)(2,1)}), bf16[1,16,2,4,16,256]{5,1,2,4,0,3:T(8,128)(2,1)}, u32[]{:S(2)}, u32[]{:S(2)}) %all-to-all-start.6) | async-done | bytes 1048608 | tf_op jit(solution)/shard_map/all_to_all | solution.py:17
  146.8 4.2 %all-to-all-start.2 = ((bf16[1,16,2,4,16,256]{5,1,2,4,0,3:T(8,128)(2,1)}), bf16[1,16,2,4,16,256]{5,1,2,4,0,3:T(8,128)(2,1)}, u32[]{:S(2)}, u32[]{:S(2)}) async-start(bf16[1,16,2,4,16,256]{5,1,2,4,0,3:T(8,128)(2,1)} %bitcast.137), calls=%async_computation.2 | async-start | bytes 2097152 | tf_op jit(solution)/shard_map/all_to_all | solution.py:17
  155.6 10.0 %all-to-all-done.2 = bf16[1,16,2,4,16,256]{5,1,2,4,0,3:T(8,128)(2,1)} async-done(((bf16[1,16,2,4,16,256]{5,1,2,4,0,3:T(8,128)(2,1)}), bf16[1,16,2,4,16,256]{5,1,2,4,0,3:T(8,128)(2,1)}, u32[]{:S(2)}, u32[]{:S(2)}) %all-to-all-start.2) | async-done | bytes 1048608 | tf_op jit(solution)/shard_map/all_to_all | solution.py:17
  165.6 4.2 %all-to-all-start.7 = ((bf16[1,16,2,4,16,256]{5,1,2,4,0,3:T(8,128)(2,1)}), bf16[1,16,2,4,16,256]{5,1,2,4,0,3:T(8,128)(2,1)}, u32[]{:S(2)}, u32[]{:S(2)}) async-start(bf16[1,16,2,4,16,256]{5,1,2,4,0,3:T(8,128)(2,1)} %bitcast.136), calls=%async_computation.7 | async-start | bytes 2097152 | tf_op jit(solution)/shard_map/all_to_all | solution.py:17
  170.1 3.6 %fusion.15 = f32[16,128,128]{2,1,0:T(8,128)} fusion(bf16[16,128,256]{2,1,0:T(8,128)(2,1)} %bitcast.150, f32[16,128,256]{2,1,0:T(8,128)} %bitcast.148), kind=kOutput, calls=%fused_computation.45 | convolution fusion | flops 138936320 | bytes 4194304 | tf_op jit(solution)/shard_map/nct,ndt->ncd/dot_general | solution.py:30
  173.7 2.4 stack.27
  176.1 2.6 fusion.16
  178.8 2.4 stack.26
  192.0 5.4 %fusion.2 = f32[4,16,16384]{2,1,0:T(8,128)} fusion(bf16[1,4,16,16384]{3,2,1,0:T(8,128)(2,1)} %param.9, f32[1,16,16384]{2,1,0:T(8,128)} %stack.28, f32[1,16,16384]{2,1,0:T(8,128)} %stack.27, f32[1,16,16384]{2,1,0:T(8,128)} %stack.26, f32[1,16,16384]{2,1,0:T(8,128)} %stack.25, f32[4,16]{1,0:T(4,128)S(1)} %shift-left_convert_fusion), kind=kLoop, calls=%fused_computation.4 | loop fusion | flops 7340032 | bytes 10486016 | tf_op jit(solution)/shard_map/jit(clip)/min | solution.py:38
  201.2 4.4 %all-to-all-start.3 = ((bf16[1,16,2,4,16,256]{5,1,2,4,0,3:T(8,128)(2,1)}), bf16[1,16,2,4,16,256]{5,1,2,4,0,3:T(8,128)(2,1)}, u32[]{:S(2)}, u32[]{:S(2)}) async-start(bf16[1,16,2,4,16,256]{5,1,2,4,0,3:T(8,128)(2,1)} %bitcast.139), calls=%async_computation.3 | async-start | bytes 2097152 | tf_op jit(solution)/shard_map/all_to_all | solution.py:17
  205.6 2.4 stack.32
  209.2 2.5 stack.33
  212.8 7.2 %all-to-all-done.3 = bf16[1,16,2,4,16,256]{5,1,2,4,0,3:T(8,128)(2,1)} async-done(((bf16[1,16,2,4,16,256]{5,1,2,4,0,3:T(8,128)(2,1)}), bf16[1,16,2,4,16,256]{5,1,2,4,0,3:T(8,128)(2,1)}, u32[]{:S(2)}, u32[]{:S(2)}) %all-to-all-start.3) | async-done | bytes 1048608 | tf_op jit(solution)/shard_map/all_to_all | solution.py:17
  225.9 1.9 subtract_convert_fusion
  227.9 56.8 %reduce-scatter.2.cloned.1.call-done = f32[4,16,2048]{2,1,0:T(8,128)} async-done(((f32[4,16,16384]{2,1,0:T(8,128)}), f32[4,16,2048]{2,1,0:T(8,128)}) %reduce-scatter.2.cloned.1.call-update) | async-done | bytes 524304 | tf_op jit(solution)/shard_map/reduce_scatter | solution.py:77
  284.7 1.9 divide_multiply_fusion
  (87 shorter events, 39.6 us)
Async XLA Ops:
  7.2 54.8 %all-gather.2.cloned.1.call-start = ((), (), s32[]{:S(2)}) async-start(), calls=%async_computation.9 | async-start | bytes 2359296 | tf_op jit(solution)/shard_map/all_gather | solution.py:46
  10.7 56.5 %all-to-all-start.4 = ((bf16[1,16,2,4,16,256]{5,4,2,1,0,3:T(8,128)(2,1)}), bf16[1,16,2,4,16,256]{5,4,2,1,0,3:T(8,128)(2,1)S(1)}, u32[]{:S(2)}, u32[]{:S(2)}) async-start(bf16[1,16,2,4,16,256]{5,4,2,1,0,3:T(8,128)(2,1)} %copy.67), calls=%async_computation.4 | async-start | bytes 2097152 | tf_op jit(solution)/shard_map/all_to_all | solution.py:17
  14.9 50.6 %copy-start = (bf16[2048,256]{1,0:T(8,128)(2,1)S(1)}, bf16[2048,256]{1,0:T(8,128)(2,1)}, u32[]{:S(2)}) copy-start(bf16[2048,256]{1,0:T(8,128)(2,1)} %param.5) | copy-start | bytes 3145732
  67.2 18.7 %all-to-all-start = ((bf16[1,16,2,4,16,256]{5,1,2,4,0,3:T(8,128)(2,1)}), bf16[1,16,2,4,16,256]{5,1,2,4,0,3:T(8,128)(2,1)}, u32[]{:S(2)}, u32[]{:S(2)}) async-start(bf16[1,16,2,4,16,256]{5,1,2,4,0,3:T(8,128)(2,1)} %bitcast.115), calls=%async_computation | async-start | bytes 2097152 | tf_op jit(solution)/shard_map/all_to_all | solution.py:17
  71.4 1.0 copy-start.21
  73.8 16.4 %copy-start.20 = (bf16[2,8,128,128]{3,1,2,0:T(8,128)(2,1)S(1)}, bf16[2,8,128,128]{3,1,2,0:T(8,128)(2,1)}, u32[]{:S(2)}) copy-start(bf16[2,8,128,128]{3,1,2,0:T(8,128)(2,1)} %get-tuple-element.6) | copy-start | bytes 1572868
  85.9 18.7 %all-to-all-start.5 = ((bf16[1,16,2,4,16,256]{5,1,2,4,0,3:T(8,128)(2,1)}), bf16[1,16,2,4,16,256]{5,1,2,4,0,3:T(8,128)(2,1)}, u32[]{:S(2)}, u32[]{:S(2)}) async-start(bf16[1,16,2,4,16,256]{5,1,2,4,0,3:T(8,128)(2,1)} %bitcast.111), calls=%async_computation.5 | async-start | bytes 2097152 | tf_op jit(solution)/shard_map/all_to_all | solution.py:17
  90.3 2.5 copy-start.12
  104.7 18.7 %all-to-all-start.1 = ((bf16[1,16,2,4,16,256]{5,1,2,4,0,3:T(8,128)(2,1)}), bf16[1,16,2,4,16,256]{5,1,2,4,0,3:T(8,128)(2,1)}, u32[]{:S(2)}, u32[]{:S(2)}) async-start(bf16[1,16,2,4,16,256]{5,1,2,4,0,3:T(8,128)(2,1)} %bitcast.138), calls=%async_computation.1 | async-start | bytes 2097152 | tf_op jit(solution)/shard_map/all_to_all | solution.py:17
  123.4 2.0 copy-start.22
  123.4 2.0 copy-start.23
  125.4 1.6 copy-start.19
  128.1 18.7 %all-to-all-start.6 = ((bf16[1,16,2,4,16,256]{5,1,2,4,0,3:T(8,128)(2,1)}), bf16[1,16,2,4,16,256]{5,1,2,4,0,3:T(8,128)(2,1)}, u32[]{:S(2)}, u32[]{:S(2)}) async-start(bf16[1,16,2,4,16,256]{5,1,2,4,0,3:T(8,128)(2,1)} %bitcast.140), calls=%async_computation.6 | async-start | bytes 2097152 | tf_op jit(solution)/shard_map/all_to_all | solution.py:17
  135.0 16.2 %copy-start.24 = (s32[4,16]{1,0:T(4,128)S(1)}, s32[4,16]{1,0:T(4,128)}, u32[]{:S(2)}) copy-start(s32[4,16]{1,0:T(4,128)} %param.8) | copy-start | bytes 772
  146.8 18.7 %all-to-all-start.2 = ((bf16[1,16,2,4,16,256]{5,1,2,4,0,3:T(8,128)(2,1)}), bf16[1,16,2,4,16,256]{5,1,2,4,0,3:T(8,128)(2,1)}, u32[]{:S(2)}, u32[]{:S(2)}) async-start(bf16[1,16,2,4,16,256]{5,1,2,4,0,3:T(8,128)(2,1)} %bitcast.137), calls=%async_computation.2 | async-start | bytes 2097152 | tf_op jit(solution)/shard_map/all_to_all | solution.py:17
  151.1 2.9 copy-start.13
  153.0 1.0 copy-start.5
  165.6 20.1 %all-to-all-start.7 = ((bf16[1,16,2,4,16,256]{5,1,2,4,0,3:T(8,128)(2,1)}), bf16[1,16,2,4,16,256]{5,1,2,4,0,3:T(8,128)(2,1)}, u32[]{:S(2)}, u32[]{:S(2)}) async-start(bf16[1,16,2,4,16,256]{5,1,2,4,0,3:T(8,128)(2,1)} %bitcast.136), calls=%async_computation.7 | async-start | bytes 2097152 | tf_op jit(solution)/shard_map/all_to_all | solution.py:17
  169.9 114.8 %reduce-scatter.2.cloned.1.call-start = ((), (), s32[]{:S(2)}) async-start(), calls=%async_computation.10 | async-start | bytes 4718592 | tf_op jit(solution)/shard_map/reduce_scatter | solution.py:77
  184.4 3.1 %copy-start.2 = (f32[16,128,128]{2,1,0:T(8,128)}, f32[16,128,128]{2,1,0:T(8,128)S(1)}, u32[]{:S(2)}) copy-start(f32[16,128,128]{2,1,0:T(8,128)S(1)} %fusion.17) | copy-start | bytes 3145732
  190.6 6.8 %copy-start.6 = (f32[16,128,128]{2,1,0:T(8,128)}, f32[16,128,128]{2,1,0:T(8,128)S(1)}, u32[]{:S(2)}) copy-start(f32[16,128,128]{2,1,0:T(8,128)S(1)} %copy.75) | copy-start | bytes 3145732
  197.3 1.2 copy-start.4
  201.2 6.8 %copy-start.1 = (f32[16,128,128]{2,1,0:T(8,128)S(1)}, f32[16,128,128]{2,1,0:T(8,128)}, u32[]{:S(2)}) copy-start(f32[16,128,128]{2,1,0:T(8,128)} %fusion.16) | copy-start | bytes 3145732
  201.2 18.9 %all-to-all-start.3 = ((bf16[1,16,2,4,16,256]{5,1,2,4,0,3:T(8,128)(2,1)}), bf16[1,16,2,4,16,256]{5,1,2,4,0,3:T(8,128)(2,1)}, u32[]{:S(2)}, u32[]{:S(2)}) async-start(bf16[1,16,2,4,16,256]{5,1,2,4,0,3:T(8,128)(2,1)} %bitcast.139), calls=%async_computation.3 | async-start | bytes 2097152 | tf_op jit(solution)/shard_map/all_to_all | solution.py:17
  209.2 2.5 copy-start.7
  212.8 9.2 %copy-start.10 = (bf16[2,8,128,128]{3,2,1,0:T(8,128)(2,1)S(1)}, bf16[2,8,128,128]{3,2,1,0:T(8,128)(2,1)}, u32[]{:S(2)}) copy-start(bf16[2,8,128,128]{3,2,1,0:T(8,128)(2,1)} %copy-done.9) | copy-start | bytes 1572868
  220.1 1.9 copy-start.14
  222.0 2.7 copy-start.16
  222.0 2.7 copy-start.17
  222.0 2.7 copy-start.18
  223.5 2.2 copy-start.8
  223.5 2.5 copy-start.15
  (3 other events, 2.6 us)
Sparse Core Ops, SparseCore 0:
  10.2 51.7 all-gather.1
  197.5 87.1 reduce-scatter.1
where the time goes:
time: 295 us; the launch traced here: 293 us
  waiting for transfers between devices  164 us (56%)
  local copies, waits for them, and re-layouts  52.9 us (18%)
  starting transfers between devices  34.4 us (12%)
  matrix products  17.1 us (6%)
  between operations  14.4 us (5%)
  other arithmetic  10.6 us (4%)
    all_to_all x8, waiting for transfers between devices, regroup(): lax.all_to_all(shaped, 'ma', split_axis=3, concat_axis=3, tiled=True)  59.6 us
    reduce_scatter x1, waiting for transfers between devices, body(): lax.psum_scatter(code_values, 'dev', scatter_dimension=2, tiled=True)  56.8 us
    all_gather x1, waiting for transfers between devices, body(): gathered = lax.all_gather(factors, 'dev', axis=2, tiled=True)  47 us
    all_to_all x8, starting transfers between devices, regroup(): lax.all_to_all(shaped, 'ma', split_axis=3, concat_axis=3, tiled=True)  34.1 us
    another operation x8, local copies, waits for them, and re-layouts, body(): jnp.stack([gradient_zero, gradient_one, gradient_two, gradient_three])  14.7 us
    all_to_all x7, local copies, waits for them, and re-layouts, regroup(): lax.all_to_all(shaped, 'ma', split_axis=3, concat_axis=3, tiled=True)  12.3 us
    unnamed x55, local copies, waits for them, and re-layouts  11.8 us
    dot_general x4, matrix products, outer_sum(): jnp.einsum('nct,ndt->ncd', left, right, preferred_element_type=jnp.float32)  8.22 us
  transfers between devices with their start and end apart: 10, of which 8 were waited for; matrix products, arithmetic and copies ran while one was open for 19% of the time, Pallas kernels for 0%

commit v1 on v0

--- a/solution.py
+++ b/solution.py
@@ -1,10 +1,33 @@
+import functools
 import jax
 import jax.numpy as jnp
 from jax import lax
 from jax.sharding import PartitionSpec as P
+from jax.lax import axis_index, axis_size, ppermute
 
 B = 128
 code_limit = 127.0
+
+
+def bring_positions_all(my_tile, named_axis):
+    n_dev_all = axis_size(named_axis)
+    windows = [my_tile]
+    k0 = 1
+    while k0 < n_dev_all:
+        windows.append(
+            ppermute(
+                windows[k0 - 1],
+                axis_name=named_axis,
+                perm=[(at, (at - 1) % n_dev_all) for at in range(n_dev_all)],
+            )
+        )
+        k0 = k0 + 1
+    extra = jnp.concatenate(windows, axis=2)
+    current_value = jnp.roll(extra, axis_index(named_axis) * my_tile.shape[2], axis=2)
+    return current_value
+
+
+trace_cards_for = functools.partial(bring_positions_all, named_axis="dev")
 
 
 def regroup(stacked):
@@ -43,7 +66,7 @@
     local_blocks = factors.shape[1]
     tok_count = inputs.shape[1]
     group_count = lax.axis_size("dev")
-    gathered = lax.all_gather(factors, "dev", axis=2, tiled=True)
+    gathered = trace_cards_for(factors)
     matrices = gathered.reshape(gathered.shape[0], local_blocks, B, B)
     block_in = inputs.reshape(local_blocks, B, tok_count)
     block_cot = cotangent.reshape(local_blocks, B, tok_count)

time: 295 us -> 311 us (1.054)
  starting transfers between devices: 34.4 us -> 65.1 us
  waiting for transfers between devices: 164 us -> 147 us
  matrix products: 17.1 us -> 22.2 us
    all_gather x1 -> x0, waiting for transfers between devices: 47 us -> none  [body(): gathered = lax.all_gather(factors, 'dev', axis=2, tiled=True)]
    ppermute x0 -> x7, starting transfers between devices: none -> 31.6 us  [bring_positions_all(): ppermute(windows[k0 - 1], axis_name=named_axis, perm=[(at, (at - 1) % n_d...]
    ppermute x0 -> x7, waiting for transfers between devices: none -> 29 us  [bring_positions_all(): ppermute(windows[k0 - 1], axis_name=named_axis, perm=[(at, (at - 1) % n_d...]
    dot_general x4, matrix products: 3.79 us -> 8.47 us  [block_backward(): jnp.einsum('ncd,ndt->nct', weights, values, preferred_element_type=jnp.fl...]
    reduce_scatter x1, waiting for transfers between devices: 56.8 us -> 60.6 us  [body(): lax.psum_scatter(code_values, 'dev', scatter_dimension=2, tiled=True)]
    unnamed x55 -> x58, local copies, waits for them, and re-layouts: 11.8 us -> 8.34 us
  transfers between devices with their start and end apart: 10 -> 16, of which waited for: 8 -> 13; matrix products, arithmetic and copies ran while one was open for 19% -> 19% of each run, Pallas kernels for 0% -> 0%
where the time goes in v1:
time: 311 us; the launch traced here: 310 us
  waiting for transfers between devices  147 us (47%)
  starting transfers between devices  65.1 us (21%)
  local copies, waits for them, and re-layouts  50.6 us (16%)
  matrix products  22.2 us (7%)
  between operations  14.5 us (5%)
  other arithmetic  10.6 us (3%)
    reduce_scatter x1, waiting for transfers between devices, body(): lax.psum_scatter(code_values, 'dev', scatter_dimension=2, tiled=True)  60.6 us
    all_to_all x8, waiting for transfers between devices, regroup(): lax.all_to_all(shaped, 'ma', split_axis=3, concat_axis=3, tiled=True)  57.1 us
    all_to_all x8, starting transfers between devices, regroup(): lax.all_to_all(shaped, 'ma', split_axis=3, concat_axis=3, tiled=True)  33.3 us
    ppermute x7, starting transfers between devices, bring_positions_all(): ppermute(windows[k0 - 1], axis_name=named_axis, perm=[(at, (at - 1) % n_d...  31.6 us
    ppermute x7, waiting for transfers between devices, bring_positions_all(): ppermute(windows[k0 - 1], axis_name=named_axis, perm=[(at, (at - 1) % n_d...  29 us
    another operation x8, local copies, waits for them, and re-layouts, body(): jnp.stack([gradient_zero, gradient_one, gradient_two, gradient_three])  16 us
    all_to_all x7, local copies, waits for them, and re-layouts, regroup(): lax.all_to_all(shaped, 'ma', split_axis=3, concat_axis=3, tiled=True)  12.3 us
    dot_general x4, matrix products, block_backward(): jnp.einsum('ncd,ndt->nct', weights, values, preferred_element_type=jnp.fl...  8.47 us
  transfers between devices with their start and end apart: 16, of which 13 were waited for; matrix products, arithmetic and copies ran while one was open for 19% of the time, Pallas kernels for 0%

profile of v1, /device:TPU:0, one launch (start us, length us, event | category | flops | bytes accessed | tf_op | source)
XLA Modules:
  0.0 309.7 jit_solution(13776655871233459892)
XLA Ops:
  7.2 6.1 %collective-permute-start = (bf16[4,16,2048]{2,1,0:T(8,128)(2,1)}, bf16[4,16,2048]{2,1,0:T(8,128)(2,1)S(1)}, u32[]{:S(2)}, u32[]{:S(2)}) collective-permute-start(bf16[4,16,2048]{2,1,0:T(8,128)(2,1)} %param.7), channel_id=1, source_target_pairs={{0,28},{4,0},{8,4},{12,8},{16,12},{20,16},{24,20},{28,24},{1,29},{... | collective-permute-start | bytes 786440 | tf_op jit(solution)/shard_map/ppermute | solution.py:18
  13.2 5.9 %collective-permute-done = bf16[4,16,2048]{2,1,0:T(8,128)(2,1)S(1)} collective-permute-done((bf16[4,16,2048]{2,1,0:T(8,128)(2,1)}, bf16[4,16,2048]{2,1,0:T(8,128)(2,1)S(1)}, u32[]{:S(2)}, u32[]{:S(2)}) %collective-permute-start) | collective-permute-done | bytes 262176 | tf_op jit(solution)/shard_map/ppermute | solution.py:18
  19.1 5.1 %collective-permute-start.1 = (bf16[4,16,2048]{2,1,0:T(8,128)(2,1)S(1)}, bf16[4,16,2048]{2,1,0:T(8,128)(2,1)S(1)}, u32[]{:S(2)}, u32[]{:S(2)}) collective-permute-start(bf16[4,16,2048]{2,1,0:T(8,128)(2,1)S(1)} %collective-permute-done), channel_id=1, source_target_pairs={{0,28},{4,0},{8,4},{12,8},{16,12},{20,16},{24,20},{28,24},{1,29},{... | collective-permute-start | bytes 786440 | tf_op jit(solution)/shard_map/ppermute | solution.py:18
  24.2 4.7 %collective-permute-done.1 = bf16[4,16,2048]{2,1,0:T(8,128)(2,1)S(1)} collective-permute-done((bf16[4,16,2048]{2,1,0:T(8,128)(2,1)S(1)}, bf16[4,16,2048]{2,1,0:T(8,128)(2,1)S(1)}, u32[]{:S(2)}, u32[]{:S(2)}) %collective-permute-start.1) | collective-permute-done | bytes 262176 | tf_op jit(solution)/shard_map/ppermute | solution.py:18
  28.9 5.2 %collective-permute-start.2 = (bf16[4,16,2048]{2,1,0:T(8,128)(2,1)S(1)}, bf16[4,16,2048]{2,1,0:T(8,128)(2,1)S(1)}, u32[]{:S(2)}, u32[]{:S(2)}) collective-permute-start(bf16[4,16,2048]{2,1,0:T(8,128)(2,1)S(1)} %collective-permute-done.1), channel_id=1, source_target_pairs={{0,28},{4,0},{8,4},{12,8},{16,12},{20,16},{24,20},{28,24},{1,29},{... | collective-permute-start | bytes 786440 | tf_op jit(solution)/shard_map/ppermute | solution.py:18
  34.1 3.9 %collective-permute-done.2 = bf16[4,16,2048]{2,1,0:T(8,128)(2,1)S(1)} collective-permute-done((bf16[4,16,2048]{2,1,0:T(8,128)(2,1)S(1)}, bf16[4,16,2048]{2,1,0:T(8,128)(2,1)S(1)}, u32[]{:S(2)}, u32[]{:S(2)}) %collective-permute-start.2) | collective-permute-done | bytes 262176 | tf_op jit(solution)/shard_map/ppermute | solution.py:18
  38.0 5.2 %collective-permute-start.3 = (bf16[4,16,2048]{2,1,0:T(8,128)(2,1)S(1)}, bf16[4,16,2048]{2,1,0:T(8,128)(2,1)S(1)}, u32[]{:S(2)}, u32[]{:S(2)}) collective-permute-start(bf16[4,16,2048]{2,1,0:T(8,128)(2,1)S(1)} %collective-permute-done.2), channel_id=1, source_target_pairs={{0,28},{4,0},{8,4},{12,8},{16,12},{20,16},{24,20},{28,24},{1,29},{... | collective-permute-start | bytes 786440 | tf_op jit(solution)/shard_map/ppermute | solution.py:18
  45.9 3.5 %all-to-all-start.4 = ((bf16[1,16,2,4,16,256]{5,4,2,1,0,3:T(8,128)(2,1)}), bf16[1,16,2,4,16,256]{5,4,2,1,0,3:T(8,128)(2,1)S(1)}, u32[]{:S(2)}, u32[]{:S(2)}) async-start(bf16[1,16,2,4,16,256]{5,4,2,1,0,3:T(8,128)(2,1)} %copy.67), calls=%async_computation.4 | async-start | bytes 2097152 | tf_op jit(solution)/shard_map/all_to_all | solution.py:40
  52.3 6.0 %collective-permute-done.4 = bf16[4,16,2048]{2,1,0:T(8,128)(2,1)S(1)} collective-permute-done((bf16[4,16,2048]{2,1,0:T(8,128)(2,1)S(1)}, bf16[4,16,2048]{2,1,0:T(8,128)(2,1)S(1)}, u32[]{:S(2)}, u32[]{:S(2)}) %collective-permute-start.4) | collective-permute-done | bytes 262176 | tf_op jit(solution)/shard_map/ppermute | solution.py:18
  58.2 3.1 collective-permute-start.5
  61.3 4.7 %collective-permute-done.5 = bf16[4,16,2048]{2,1,0:T(8,128)(2,1)S(1)} collective-permute-done((bf16[4,16,2048]{2,1,0:T(8,128)(2,1)S(1)}, bf16[4,16,2048]{2,1,0:T(8,128)(2,1)S(1)}, u32[]{:S(2)}, u32[]{:S(2)}) %collective-permute-start.5) | collective-permute-done | bytes 262176 | tf_op jit(solution)/shard_map/ppermute | solution.py:18
  66.0 4.3 %collective-permute-start.6 = (bf16[4,16,2048]{2,1,0:T(8,128)(2,1)S(1)}, bf16[4,16,2048]{2,1,0:T(8,128)(2,1)S(1)}, u32[]{:S(2)}, u32[]{:S(2)}) collective-permute-start(bf16[4,16,2048]{2,1,0:T(8,128)(2,1)S(1)} %collective-permute-done.5), channel_id=1, source_target_pairs={{0,28},{4,0},{8,4},{12,8},{16,12},{20,16},{24,20},{28,24},{1,29},{... | collective-permute-start | bytes 786440 | tf_op jit(solution)/shard_map/ppermute | solution.py:18
  70.4 3.8 %collective-permute-done.6 = bf16[4,16,2048]{2,1,0:T(8,128)(2,1)S(1)} collective-permute-done((bf16[4,16,2048]{2,1,0:T(8,128)(2,1)S(1)}, bf16[4,16,2048]{2,1,0:T(8,128)(2,1)S(1)}, u32[]{:S(2)}, u32[]{:S(2)}) %collective-permute-start.6) | collective-permute-done | bytes 262176 | tf_op jit(solution)/shard_map/ppermute | solution.py:18
  78.2 4.2 %all-to-all-start = ((bf16[1,16,2,4,16,256]{5,1,2,4,0,3:T(8,128)(2,1)}), bf16[1,16,2,4,16,256]{5,1,2,4,0,3:T(8,128)(2,1)}, u32[]{:S(2)}, u32[]{:S(2)}) async-start(bf16[1,16,2,4,16,256]{5,1,2,4,0,3:T(8,128)(2,1)} %bitcast.92), calls=%async_computation | async-start | bytes 2097152 | tf_op jit(solution)/shard_map/all_to_all | solution.py:40
  86.1 10.8 %all-to-all-done = bf16[1,16,2,4,16,256]{5,1,2,4,0,3:T(8,128)(2,1)} async-done(((bf16[1,16,2,4,16,256]{5,1,2,4,0,3:T(8,128)(2,1)}), bf16[1,16,2,4,16,256]{5,1,2,4,0,3:T(8,128)(2,1)}, u32[]{:S(2)}, u32[]{:S(2)}) %all-to-all-start) | async-done | bytes 1048608 | tf_op jit(solution)/shard_map/all_to_all | solution.py:40
  96.9 4.2 %all-to-all-start.5 = ((bf16[1,16,2,4,16,256]{5,1,2,4,0,3:T(8,128)(2,1)}), bf16[1,16,2,4,16,256]{5,1,2,4,0,3:T(8,128)(2,1)}, u32[]{:S(2)}, u32[]{:S(2)}) async-start(bf16[1,16,2,4,16,256]{5,1,2,4,0,3:T(8,128)(2,1)} %bitcast.88), calls=%async_computation.5 | async-start | bytes 2097152 | tf_op jit(solution)/shard_map/all_to_all | solution.py:40
  104.9 10.8 %all-to-all-done.5 = bf16[1,16,2,4,16,256]{5,1,2,4,0,3:T(8,128)(2,1)} async-done(((bf16[1,16,2,4,16,256]{5,1,2,4,0,3:T(8,128)(2,1)}), bf16[1,16,2,4,16,256]{5,1,2,4,0,3:T(8,128)(2,1)}, u32[]{:S(2)}, u32[]{:S(2)}) %all-to-all-start.5) | async-done | bytes 1048608 | tf_op jit(solution)/shard_map/all_to_all | solution.py:40
  115.7 4.2 %all-to-all-start.1 = ((bf16[1,16,2,4,16,256]{5,1,2,4,0,3:T(8,128)(2,1)}), bf16[1,16,2,4,16,256]{5,1,2,4,0,3:T(8,128)(2,1)}, u32[]{:S(2)}, u32[]{:S(2)}) async-start(bf16[1,16,2,4,16,256]{5,1,2,4,0,3:T(8,128)(2,1)} %bitcast.115), calls=%async_computation.1 | async-start | bytes 2097152 | tf_op jit(solution)/shard_map/all_to_all | solution.py:40
  121.8 2.8 copy.70
  124.6 9.8 %all-to-all-done.1 = bf16[1,16,2,4,16,256]{5,1,2,4,0,3:T(8,128)(2,1)} async-done(((bf16[1,16,2,4,16,256]{5,1,2,4,0,3:T(8,128)(2,1)}), bf16[1,16,2,4,16,256]{5,1,2,4,0,3:T(8,128)(2,1)}, u32[]{:S(2)}, u32[]{:S(2)}) %all-to-all-start.1) | async-done | bytes 1048608 | tf_op jit(solution)/shard_map/all_to_all | solution.py:40
  136.3 3.7 %fusion.9 = bf16[16,128,256]{2,1,0:T(8,128)(2,1)S(1)} fusion(f32[16,128,256]{2,1,0:T(8,128)S(1)} %bitcast.123, bf16[16,128,128]{2,1,0:T(8,128)(2,1)} %bitcast.131, bf16[16,128,256]{2,1,0:T(8,128)(2,1)} %bitcast.127), kind=kOutput, calls=%fused_computation.14 | convolution fusion | flops 144703488 | bytes 4718592 | tf_op jit(solution)/shard_map/ncd,ndt->nct/dot_general | solution.py:49
  141.1 4.2 %all-to-all-start.6 = ((bf16[1,16,2,4,16,256]{5,1,2,4,0,3:T(8,128)(2,1)}), bf16[1,16,2,4,16,256]{5,1,2,4,0,3:T(8,128)(2,1)}, u32[]{:S(2)}, u32[]{:S(2)}) async-start(bf16[1,16,2,4,16,256]{5,1,2,4,0,3:T(8,128)(2,1)} %bitcast.117), calls=%async_computation.6 | async-start | bytes 2097152 | tf_op jit(solution)/shard_map/all_to_all | solution.py:40
  149.1 10.7 %all-to-all-done.6 = bf16[1,16,2,4,16,256]{5,1,2,4,0,3:T(8,128)(2,1)} async-done(((bf16[1,16,2,4,16,256]{5,1,2,4,0,3:T(8,128)(2,1)}), bf16[1,16,2,4,16,256]{5,1,2,4,0,3:T(8,128)(2,1)}, u32[]{:S(2)}, u32[]{:S(2)}) %all-to-all-start.6) | async-done | bytes 1048608 | tf_op jit(solution)/shard_map/all_to_all | solution.py:40
  159.8 4.3 %all-to-all-start.2 = ((bf16[1,16,2,4,16,256]{5,1,2,4,0,3:T(8,128)(2,1)}), bf16[1,16,2,4,16,256]{5,1,2,4,0,3:T(8,128)(2,1)}, u32[]{:S(2)}, u32[]{:S(2)}) async-start(bf16[1,16,2,4,16,256]{5,1,2,4,0,3:T(8,128)(2,1)} %bitcast.114), calls=%async_computation.2 | async-start | bytes 2097152 | tf_op jit(solution)/shard_map/all_to_all | solution.py:40
  169.5 9.1 %all-to-all-done.2 = bf16[1,16,2,4,16,256]{5,1,2,4,0,3:T(8,128)(2,1)} async-done(((bf16[1,16,2,4,16,256]{5,1,2,4,0,3:T(8,128)(2,1)}), bf16[1,16,2,4,16,256]{5,1,2,4,0,3:T(8,128)(2,1)}, u32[]{:S(2)}, u32[]{:S(2)}) %all-to-all-start.2) | async-done | bytes 1048608 | tf_op jit(solution)/shard_map/all_to_all | solution.py:40
  178.6 4.2 %all-to-all-start.7 = ((bf16[1,16,2,4,16,256]{5,1,2,4,0,3:T(8,128)(2,1)}), bf16[1,16,2,4,16,256]{5,1,2,4,0,3:T(8,128)(2,1)}, u32[]{:S(2)}, u32[]{:S(2)}) async-start(bf16[1,16,2,4,16,256]{5,1,2,4,0,3:T(8,128)(2,1)} %bitcast.113), calls=%async_computation.7 | async-start | bytes 2097152 | tf_op jit(solution)/shard_map/all_to_all | solution.py:40
  183.0 3.6 %fusion.12 = f32[16,128,128]{2,1,0:T(8,128)} fusion(bf16[16,128,256]{2,1,0:T(8,128)(2,1)} %bitcast.128, f32[16,128,256]{2,1,0:T(8,128)} %bitcast.125), kind=kOutput, calls=%fused_computation.56 | convolution fusion | flops 138936320 | bytes 4194304 | tf_op jit(solution)/shard_map/nct,ndt->ncd/dot_general | solution.py:53
  204.9 5.4 %fusion.2 = f32[4,16,16384]{2,1,0:T(8,128)} fusion(bf16[1,4,16,16384]{3,2,1,0:T(8,128)(2,1)} %param.9, f32[1,16,16384]{2,1,0:T(8,128)} %stack.28, f32[1,16,16384]{2,1,0:T(8,128)} %stack.27, f32[1,16,16384]{2,1,0:T(8,128)} %stack.26, f32[1,16,16384]{2,1,0:T(8,128)} %stack.25, f32[4,16]{1,0:T(4,128)S(1)} %shift-left_convert_fusion), kind=kLoop, calls=%fused_computation.4 | loop fusion | flops 7340032 | bytes 10486016 | tf_op jit(solution)/shard_map/jit(clip)/min | solution.py:61
  213.3 4.3 %all-to-all-start.3 = ((bf16[1,16,2,4,16,256]{5,1,2,4,0,3:T(8,128)(2,1)}), bf16[1,16,2,4,16,256]{5,1,2,4,0,3:T(8,128)(2,1)}, u32[]{:S(2)}, u32[]{:S(2)}) async-start(bf16[1,16,2,4,16,256]{5,1,2,4,0,3:T(8,128)(2,1)} %bitcast.116), calls=%async_computation.3 | async-start | bytes 2097152 | tf_op jit(solution)/shard_map/all_to_all | solution.py:40
  226.1 6.0 %all-to-all-done.3 = bf16[1,16,2,4,16,256]{5,1,2,4,0,3:T(8,128)(2,1)} async-done(((bf16[1,16,2,4,16,256]{5,1,2,4,0,3:T(8,128)(2,1)}), bf16[1,16,2,4,16,256]{5,1,2,4,0,3:T(8,128)(2,1)}, u32[]{:S(2)}, u32[]{:S(2)}) %all-to-all-start.3) | async-done | bytes 1048608 | tf_op jit(solution)/shard_map/all_to_all | solution.py:40
  234.1 2.9 fusion.10
  240.3 60.6 %reduce-scatter.2.cloned.1.call-done = f32[4,16,2048]{2,1,0:T(8,128)} async-done(((f32[4,16,16384]{2,1,0:T(8,128)}), f32[4,16,2048]{2,1,0:T(8,128)}) %reduce-scatter.2.cloned.1.call-update) | async-done | bytes 524304 | tf_op jit(solution)/shard_map/reduce_scatter | solution.py:100
  (102 shorter events, 68.0 us)
Async XLA Ops:
  7.2 42.3 %copy-start.17 = (bf16[4,16,2048]{2,1,0:T(8,128)(2,1)S(1)}, bf16[4,16,2048]{2,1,0:T(8,128)(2,1)}, u32[]{:S(2)}) copy-start(bf16[4,16,2048]{2,1,0:T(8,128)(2,1)} %param.7) | copy-start | bytes 786436
  7.2 11.9 %collective-permute-start = (bf16[4,16,2048]{2,1,0:T(8,128)(2,1)}, bf16[4,16,2048]{2,1,0:T(8,128)(2,1)S(1)}, u32[]{:S(2)}, u32[]{:S(2)}) collective-permute-start(bf16[4,16,2048]{2,1,0:T(8,128)(2,1)} %param.7), channel_id=1, source_target_pairs={{0,28},{4,0},{8,4},{12,8},{16,12},{20,16},{24,20},{28,24},{1,29},{... | collective-permute-start | bytes 786440 | tf_op jit(solution)/shard_map/ppermute | solution.py:18
  19.1 9.8 %collective-permute-start.1 = (bf16[4,16,2048]{2,1,0:T(8,128)(2,1)S(1)}, bf16[4,16,2048]{2,1,0:T(8,128)(2,1)S(1)}, u32[]{:S(2)}, u32[]{:S(2)}) collective-permute-start(bf16[4,16,2048]{2,1,0:T(8,128)(2,1)S(1)} %collective-permute-done), channel_id=1, source_target_pairs={{0,28},{4,0},{8,4},{12,8},{16,12},{20,16},{24,20},{28,24},{1,29},{... | collective-permute-start | bytes 786440 | tf_op jit(solution)/shard_map/ppermute | solution.py:18
  28.9 9.1 %collective-permute-start.2 = (bf16[4,16,2048]{2,1,0:T(8,128)(2,1)S(1)}, bf16[4,16,2048]{2,1,0:T(8,128)(2,1)S(1)}, u32[]{:S(2)}, u32[]{:S(2)}) collective-permute-start(bf16[4,16,2048]{2,1,0:T(8,128)(2,1)S(1)} %collective-permute-done.1), channel_id=1, source_target_pairs={{0,28},{4,0},{8,4},{12,8},{16,12},{20,16},{24,20},{28,24},{1,29},{... | collective-permute-start | bytes 786440 | tf_op jit(solution)/shard_map/ppermute | solution.py:18
  38.0 11.5 %collective-permute-start.3 = (bf16[4,16,2048]{2,1,0:T(8,128)(2,1)S(1)}, bf16[4,16,2048]{2,1,0:T(8,128)(2,1)S(1)}, u32[]{:S(2)}, u32[]{:S(2)}) collective-permute-start(bf16[4,16,2048]{2,1,0:T(8,128)(2,1)S(1)} %collective-permute-done.2), channel_id=1, source_target_pairs={{0,28},{4,0},{8,4},{12,8},{16,12},{20,16},{24,20},{28,24},{1,29},{... | collective-permute-start | bytes 786440 | tf_op jit(solution)/shard_map/ppermute | solution.py:18
  45.9 32.2 %all-to-all-start.4 = ((bf16[1,16,2,4,16,256]{5,4,2,1,0,3:T(8,128)(2,1)}), bf16[1,16,2,4,16,256]{5,4,2,1,0,3:T(8,128)(2,1)S(1)}, u32[]{:S(2)}, u32[]{:S(2)}) async-start(bf16[1,16,2,4,16,256]{5,4,2,1,0,3:T(8,128)(2,1)} %copy.67), calls=%async_computation.4 | async-start | bytes 2097152 | tf_op jit(solution)/shard_map/all_to_all | solution.py:40
  49.5 8.7 %collective-permute-start.4 = (bf16[4,16,2048]{2,1,0:T(8,128)(2,1)S(1)}, bf16[4,16,2048]{2,1,0:T(8,128)(2,1)S(1)}, u32[]{:S(2)}, u32[]{:S(2)}) collective-permute-start(bf16[4,16,2048]{2,1,0:T(8,128)(2,1)S(1)} %collective-permute-done.3), channel_id=1, source_target_pairs={{0,28},{4,0},{8,4},{12,8},{16,12},{20,16},{24,20},{28,24},{1,29},{... | collective-permute-start | bytes 786440 | tf_op jit(solution)/shard_map/ppermute | solution.py:18
  58.2 7.8 %collective-permute-start.5 = (bf16[4,16,2048]{2,1,0:T(8,128)(2,1)S(1)}, bf16[4,16,2048]{2,1,0:T(8,128)(2,1)S(1)}, u32[]{:S(2)}, u32[]{:S(2)}) collective-permute-start(bf16[4,16,2048]{2,1,0:T(8,128)(2,1)S(1)} %collective-permute-done.4), channel_id=1, source_target_pairs={{0,28},{4,0},{8,4},{12,8},{16,12},{20,16},{24,20},{28,24},{1,29},{... | collective-permute-start | bytes 786440 | tf_op jit(solution)/shard_map/ppermute | solution.py:18
  66.0 8.2 %collective-permute-start.6 = (bf16[4,16,2048]{2,1,0:T(8,128)(2,1)S(1)}, bf16[4,16,2048]{2,1,0:T(8,128)(2,1)S(1)}, u32[]{:S(2)}, u32[]{:S(2)}) collective-permute-start(bf16[4,16,2048]{2,1,0:T(8,128)(2,1)S(1)} %collective-permute-done.5), channel_id=1, source_target_pairs={{0,28},{4,0},{8,4},{12,8},{16,12},{20,16},{24,20},{28,24},{1,29},{... | collective-permute-start | bytes 786440 | tf_op jit(solution)/shard_map/ppermute | solution.py:18
  74.3 2.2 copy-start
  78.2 18.7 %all-to-all-start = ((bf16[1,16,2,4,16,256]{5,1,2,4,0,3:T(8,128)(2,1)}), bf16[1,16,2,4,16,256]{5,1,2,4,0,3:T(8,128)(2,1)}, u32[]{:S(2)}, u32[]{:S(2)}) async-start(bf16[1,16,2,4,16,256]{5,1,2,4,0,3:T(8,128)(2,1)} %bitcast.92), calls=%async_computation | async-start | bytes 2097152 | tf_op jit(solution)/shard_map/all_to_all | solution.py:40
  82.6 18.6 %copy-start.16 = (bf16[2,8,128,128]{3,1,2,0:T(8,128)(2,1)S(1)}, bf16[2,8,128,128]{3,1,2,0:T(8,128)(2,1)}, u32[]{:S(2)}) copy-start(bf16[2,8,128,128]{3,1,2,0:T(8,128)(2,1)} %get-tuple-element.5) | copy-start | bytes 1572868
  96.9 18.7 %all-to-all-start.5 = ((bf16[1,16,2,4,16,256]{5,1,2,4,0,3:T(8,128)(2,1)}), bf16[1,16,2,4,16,256]{5,1,2,4,0,3:T(8,128)(2,1)}, u32[]{:S(2)}, u32[]{:S(2)}) async-start(bf16[1,16,2,4,16,256]{5,1,2,4,0,3:T(8,128)(2,1)} %bitcast.88), calls=%async_computation.5 | async-start | bytes 2097152 | tf_op jit(solution)/shard_map/all_to_all | solution.py:40
  101.3 2.0 copy-start.10
  115.7 18.7 %all-to-all-start.1 = ((bf16[1,16,2,4,16,256]{5,1,2,4,0,3:T(8,128)(2,1)}), bf16[1,16,2,4,16,256]{5,1,2,4,0,3:T(8,128)(2,1)}, u32[]{:S(2)}, u32[]{:S(2)}) async-start(bf16[1,16,2,4,16,256]{5,1,2,4,0,3:T(8,128)(2,1)} %bitcast.115), calls=%async_computation.1 | async-start | bytes 2097152 | tf_op jit(solution)/shard_map/all_to_all | solution.py:40
  136.2 3.7 %copy-start.15 = (f32[1,16,2,4,16,256]{5,4,3,2,1,0:T(8,128)}, f32[1,16,2,4,16,256]{5,4,3,2,1,0:T(8,128)S(1)}, u32[]{:S(2)}) copy-start(f32[1,16,2,4,16,256]{5,4,3,2,1,0:T(8,128)S(1)} %copy.60) | copy-start | bytes 6291460
  141.1 18.7 %all-to-all-start.6 = ((bf16[1,16,2,4,16,256]{5,1,2,4,0,3:T(8,128)(2,1)}), bf16[1,16,2,4,16,256]{5,1,2,4,0,3:T(8,128)(2,1)}, u32[]{:S(2)}, u32[]{:S(2)}) async-start(bf16[1,16,2,4,16,256]{5,1,2,4,0,3:T(8,128)(2,1)} %bitcast.117), calls=%async_computation.6 | async-start | bytes 2097152 | tf_op jit(solution)/shard_map/all_to_all | solution.py:40
  145.3 18.8 %copy-start.18 = (s32[4,16]{1,0:T(4,128)S(1)}, s32[4,16]{1,0:T(4,128)}, u32[]{:S(2)}) copy-start(s32[4,16]{1,0:T(4,128)} %param.8) | copy-start | bytes 772
  159.8 18.8 %all-to-all-start.2 = ((bf16[1,16,2,4,16,256]{5,1,2,4,0,3:T(8,128)(2,1)}), bf16[1,16,2,4,16,256]{5,1,2,4,0,3:T(8,128)(2,1)}, u32[]{:S(2)}, u32[]{:S(2)}) async-start(bf16[1,16,2,4,16,256]{5,1,2,4,0,3:T(8,128)(2,1)} %bitcast.114), calls=%async_computation.2 | async-start | bytes 2097152 | tf_op jit(solution)/shard_map/all_to_all | solution.py:40
  165.9 1.0 copy-start.4
  178.6 20.2 %all-to-all-start.7 = ((bf16[1,16,2,4,16,256]{5,1,2,4,0,3:T(8,128)(2,1)}), bf16[1,16,2,4,16,256]{5,1,2,4,0,3:T(8,128)(2,1)}, u32[]{:S(2)}, u32[]{:S(2)}) async-start(bf16[1,16,2,4,16,256]{5,1,2,4,0,3:T(8,128)(2,1)} %bitcast.113), calls=%async_computation.7 | async-start | bytes 2097152 | tf_op jit(solution)/shard_map/all_to_all | solution.py:40
  182.8 118.1 %reduce-scatter.2.cloned.1.call-start = ((), (), s32[]{:S(2)}) async-start(), calls=%async_computation.9 | async-start | bytes 4718592 | tf_op jit(solution)/shard_map/reduce_scatter | solution.py:100
  197.4 1.3 copy-start.2
  203.5 6.7 %copy-start.5 = (f32[16,128,128]{2,1,0:T(8,128)}, f32[16,128,128]{2,1,0:T(8,128)S(1)}, u32[]{:S(2)}) copy-start(f32[16,128,128]{2,1,0:T(8,128)S(1)} %copy.75) | copy-start | bytes 3145732
  210.3 9.8 %copy-start.1 = (f32[16,128,128]{2,1,0:T(8,128)S(1)}, f32[16,128,128]{2,1,0:T(8,128)}, u32[]{:S(2)}) copy-start(f32[16,128,128]{2,1,0:T(8,128)} %fusion.14) | copy-start | bytes 3145732
  213.3 18.8 %all-to-all-start.3 = ((bf16[1,16,2,4,16,256]{5,1,2,4,0,3:T(8,128)(2,1)}), bf16[1,16,2,4,16,256]{5,1,2,4,0,3:T(8,128)(2,1)}, u32[]{:S(2)}, u32[]{:S(2)}) async-start(bf16[1,16,2,4,16,256]{5,1,2,4,0,3:T(8,128)(2,1)} %bitcast.116), calls=%async_computation.3 | async-start | bytes 2097152 | tf_op jit(solution)/shard_map/all_to_all | solution.py:40
  221.3 12.8 %copy-start.8 = (bf16[2,8,128,128]{3,2,1,0:T(8,128)(2,1)S(1)}, bf16[2,8,128,128]{3,2,1,0:T(8,128)(2,1)}, u32[]{:S(2)}) copy-start(bf16[2,8,128,128]{3,2,1,0:T(8,128)(2,1)} %copy-done.7) | copy-start | bytes 1572868
  232.1 6.2 %copy-start.6 = (bf16[1,4,16,16384]{3,2,1,0:T(8,128)(2,1)S(1)}, bf16[1,4,16,16384]{3,2,1,0:T(8,128)(2,1)}, u32[]{:S(2)}) copy-start(bf16[1,4,16,16384]{3,2,1,0:T(8,128)(2,1)} %param.9) | copy-start | bytes 6291460
  232.1 6.2 %copy-start.11 = (f32[1,1,16,16384]{3,2,1,0:T(8,128)S(1)}, f32[1,1,16,16384]{3,2,1,0:T(8,128)}, u32[]{:S(2)}) copy-start(f32[1,1,16,16384]{3,2,1,0:T(8,128)} %stack.32) | copy-start | bytes 3145732
  232.1 6.2 %copy-start.12 = (f32[1,1,16,16384]{3,2,1,0:T(8,128)S(1)}, f32[1,1,16,16384]{3,2,1,0:T(8,128)}, u32[]{:S(2)}) copy-start(f32[1,1,16,16384]{3,2,1,0:T(8,128)} %stack.33) | copy-start | bytes 3145732
  232.1 6.2 %copy-start.13 = (f32[1,1,16,16384]{3,2,1,0:T(8,128)S(1)}, f32[1,1,16,16384]{3,2,1,0:T(8,128)}, u32[]{:S(2)}) copy-start(f32[1,1,16,16384]{3,2,1,0:T(8,128)} %stack.31) | copy-start | bytes 3145732
  232.1 6.2 %copy-start.14 = (f32[1,1,16,16384]{3,2,1,0:T(8,128)S(1)}, f32[1,1,16,16384]{3,2,1,0:T(8,128)}, u32[]{:S(2)}) copy-start(f32[1,1,16,16384]{3,2,1,0:T(8,128)} %stack.30) | copy-start | bytes 3145732
  (3 other events, 2.6 us)
Sparse Core Ops, SparseCore 0:
  210.4 90.4 reduce-scatter.1
